TPU v7x, 32 devices: a whole 2x2x4 slice. The times are simulated.
32 devices in a mesh: group: 4 (over x, core), ctx: 8 (over z, y).
Axes of the slice: x: 2, y: 2, z: 4, core: 2. Of those that a mesh axis runs over, the one named last changes fastest.
Arguments:
- query_rows: bfloat16 [4, 2048, 4096], P('group', 'ctx'), may hold values from -250 to 250
- key_rows: bfloat16 [4, 2048, 512], P('group', 'ctx'), may hold values from -7 to 7
- value_rows: bfloat16 [4, 2048, 512], P('group', 'ctx'), may hold values from -6 to 6
- documents: int32 [4, 2048], P('group', 'ctx'), may hold values from 0 to 3, never falling along the last dimension, each value on 1 to 1280 neighbouring positions
- owners: int32 [4, 64, 1], P('group', 'ctx'), may hold values from 0 to 3; in each aligned block of 8 rows (0 to 7, 8 to 15, ..., all dimensions but the last counted through in order) at most 2 rows name the same one
Outputs:
- attended: bfloat16 [4, 2048, 4096], P('group', 'ctx')
- page_pool: bfloat16 [4, 64, 2, 128, 128], P('group', 'ctx')
- page_scales: bfloat16 [4, 64, 2], P('group', 'ctx')
Inputs may be any that keep to these rules, and one draw needn't show every extreme that they name: `documents`: document numbers never fall along a group's tokens; each document has at most 1280 tokens. `owners`: among the pages of one device, no owner is named more than 2 times.
All inputs are finite; a program needn't handle non-finite values.
Results may differ from a plain program's by a relative error of at most 0.0028.
Values may be sent and summed in bfloat16 or wider, within the bound.
A program may use at most 128 MiB of HBM per device.

v0:
```python
import math

import jax
import jax.numpy as jnp
from jax import lax
from jax.sharding import PartitionSpec as P

E = 128
HQ = 32
HK = 4
PAGE = 128


epsilon = 1e-06
masked_score = -1e30


def split_heads(queries_here, keys_here, values_here, doc_marks):
    tokens = queries_here.shape[0]
    ctx_count = lax.axis_size("ctx")
    per_device = HQ // ctx_count
    score_scale = 1.0 / math.sqrt(E)
    kv_pairs = jnp.stack(
        [keys_here.reshape(tokens, HK, E), values_here.reshape(tokens, HK, E)], axis=2
    )
    spread = jnp.repeat(kv_pairs, ctx_count // HK, axis=1)
    spread_marks = jnp.broadcast_to(doc_marks[:, None], (tokens, ctx_count))
    all_pairs, all_marks = (
        lax.all_to_all(spread, "ctx", split_axis=1, concat_axis=0, tiled=True),
        lax.all_to_all(spread_marks, "ctx", split_axis=1, concat_axis=0, tiled=True),
    )
    key_all = all_pairs[:, 0, 0]
    value_all = all_pairs[:, 0, 1]
    marks_all = all_marks[:, 0]
    length = key_all.shape[0]
    key_pos = jnp.arange(length, dtype=jnp.int32)
    block_rows = math.gcd(length, 512)
    shaped = queries_here.reshape(tokens, ctx_count, per_device, E)
    head_rows = lax.all_to_all(shaped, "ctx", split_axis=1, concat_axis=0, tiled=True)[:, 0]
    head_count = head_rows.shape[1]

    def one_block(block_index):
        first_row = block_index * block_rows
        query_block = lax.dynamic_slice_in_dim(head_rows, first_row, block_rows, 0)
        mark_rows = lax.dynamic_slice_in_dim(marks_all, first_row, block_rows, 0)
        query_pos = first_row + jnp.arange(block_rows, dtype=jnp.int32)
        scores = (
            jnp.einsum("qhe,ke->hqk", query_block, key_all, preferred_element_type=jnp.float32)
            * score_scale
        )
        visible = (mark_rows[:, None] == marks_all[None, :]) & (
            query_pos[:, None] >= key_pos[None, :]
        )
        scores = jnp.where(visible, scores, masked_score)
        largest = jnp.max(scores, axis=-1, keepdims=True)
        weights = jnp.exp(scores - largest)
        totals = jnp.sum(weights, axis=-1)
        weighted = jnp.einsum(
            "hqk,ke->qhe",
            weights.astype(jnp.bfloat16),
            value_all,
            preferred_element_type=jnp.float32,
        )
        return (weighted / jnp.transpose(totals)[..., None]).astype(jnp.bfloat16)

    blocks = lax.map(one_block, jnp.arange(length // block_rows, dtype=jnp.int32))
    result = blocks.reshape(length, 1, head_count, E)
    merged = lax.all_to_all(result, "ctx", split_axis=0, concat_axis=1, tiled=True)
    return merged.reshape(tokens, HQ * E)


def deliver_pages(keys_here, values_here, owner_list):
    tokens = keys_here.shape[0]
    block_count = tokens // PAGE
    key_pages = keys_here.reshape(block_count, PAGE, HK, E).transpose(0, 2, 1, 3)
    value_pages = values_here.reshape(block_count, PAGE, HK, E).transpose(0, 2, 1, 3)
    page_count = block_count * HK
    kv_pairs = jnp.stack([key_pages, value_pages], axis=2).reshape(page_count, 2, PAGE, E)
    magnitude = jnp.max(jnp.abs(kv_pairs.astype(jnp.float32)), axis=(2, 3)) + epsilon
    scales = magnitude.astype(jnp.bfloat16)
    stored = (kv_pairs.astype(jnp.float32) / scales.astype(jnp.float32)[:, :, None, None]).astype(
        jnp.bfloat16
    )
    groups_n = lax.axis_size("group")
    slot_depth = max(2, (page_count + groups_n - 1) // groups_n)
    page_order = jnp.arange(page_count, dtype=jnp.int32)
    earlier = (owner_list[:, None] == owner_list[None, :]) & (
        page_order[None, :] < page_order[:, None]
    )
    page_rank = jnp.sum(earlier.astype(jnp.int32), axis=1)
    slot_of = owner_list * slot_depth + page_rank
    select = (
        jnp.arange(groups_n * slot_depth, dtype=jnp.int32)[:, None] == slot_of[None, :]
    ).astype(jnp.bfloat16)
    packed = jnp.dot(
        select, stored.reshape(page_count, 2 * PAGE * E), preferred_element_type=jnp.float32
    ).astype(jnp.bfloat16)
    packed_scales = jnp.dot(select, scales, preferred_element_type=jnp.float32).astype(jnp.bfloat16)
    packed = packed.reshape(groups_n, slot_depth, 2, PAGE, E)
    packed_scales = packed_scales.reshape(groups_n, slot_depth, 2)
    arrived, arrived_scales = (
        lax.all_to_all(packed, "group", split_axis=0, concat_axis=0, tiled=True),
        lax.all_to_all(packed_scales, "group", split_axis=0, concat_axis=0, tiled=True),
    )
    return (
        arrived.reshape(1, groups_n * slot_depth, 2, PAGE, E),
        arrived_scales.reshape(1, groups_n * slot_depth, 2),
    )


def local(query_rows, key_rows, value_rows, documents, owners):
    queries_here = query_rows[0]
    keys_here = key_rows[0]
    values_here = value_rows[0]
    doc_marks = documents[0].astype(jnp.bfloat16)
    attended = split_heads(queries_here, keys_here, values_here, doc_marks)
    page_pool, page_scales = deliver_pages(keys_here, values_here, owners[0, :, 0])
    return (attended[None], page_pool, page_scales)


def solution(mesh):
    placed = (
        P("group", "ctx", None),
        P("group", "ctx", None),
        P("group", "ctx", None),
        P("group", "ctx"),
        P("group", "ctx", None),
    )
    return jax.shard_map(
        local,
        mesh=mesh,
        in_specs=placed,
        out_specs=(
            P("group", "ctx", None),
            P("group", "ctx", None, None, None),
            P("group", "ctx", None),
        ),
        check_vma=False,
    )
```

profile of v0, /device:TPU:28, one launch (start us, length us, event | category | flops | bytes accessed | tf_op | source)
XLA Modules:
  0.0 239.3 jit_solution(9955925464402207372)
XLA Ops:
  3.1 6.0 %all-to-all-start = ((bf16[8,2,128]{2,1,0:T(2,128)(2,1)}), bf16[8,2,128]{2,1,0:T(2,128)(2,1)S(1)}, u32[]{:S(2)}, u32[]{:S(2)}) async-start(bf16[8,2,128]{2,1,0:T(2,128)(2,1)} %reshape.89), calls=%async_computation | async-start | bytes 8192 | tf_op jit(solution)/shard_map/all_to_all | solution.py:30
  12.8 7.4 %all-to-all-start.2 = ((bf16[256,8,2,128]{3,0,2,1:T(8,128)(2,1)}), bf16[256,8,2,128]{3,0,2,1:T(8,128)(2,1)S(1)}, u32[]{:S(2)}, u32[]{:S(2)}) async-start(bf16[256,8,2,128]{3,0,2,1:T(8,128)(2,1)} %bitcast.6), calls=%async_computation.2 | async-start | bytes 2097152 | tf_op jit(solution)/shard_map/all_to_all | solution.py:29
  20.2 3.3 %copy.47 = bf16[1,256,4096]{1,2,0:T(8,128)(2,1)S(1)} copy(bf16[1,256,4096]{2,1,0:T(8,128)(2,1)} %param.7) | data formatting | bytes 4194304 | tf_op args[0]
  23.5 2.4 %copy.48 = bf16[256,8,4,128]{3,0,2,1:T(8,128)(2,1)} copy(bf16[256,8,4,128]{0,3,2,1:T(8,128)(2,1)S(1)} %bitcast.113) | data formatting | bytes 4194304 | tf_op jit(solution)/shard_map/reshape;squeeze | solution.py:38
  25.9 16.5 %all-to-all-done.2 = bf16[256,8,2,128]{3,0,2,1:T(8,128)(2,1)S(1)} async-done(((bf16[256,8,2,128]{3,0,2,1:T(8,128)(2,1)}), bf16[256,8,2,128]{3,0,2,1:T(8,128)(2,1)S(1)}, u32[]{:S(2)}, u32[]{:S(2)}) %all-to-all-start.2) | async-done | bytes 1048608 | tf_op jit(solution)/shard_map/all_to_all | solution.py:29
  42.4 6.1 %all-to-all-start.1 = ((bf16[256,8,4,128]{3,0,2,1:T(8,128)(2,1)}), bf16[256,8,4,128]{3,0,2,1:T(8,128)(2,1)S(1)}, u32[]{:S(2)}, u32[]{:S(2)}) async-start(bf16[256,8,4,128]{3,0,2,1:T(8,128)(2,1)} %copy.48), calls=%async_computation.1 | async-start | bytes 4194304 | tf_op jit(solution)/shard_map/all_to_all | solution.py:39
  55.2 39.3 %all-to-all-done.1 = bf16[256,8,4,128]{3,0,2,1:T(8,128)(2,1)S(1)} async-done(((bf16[256,8,4,128]{3,0,2,1:T(8,128)(2,1)}), bf16[256,8,4,128]{3,0,2,1:T(8,128)(2,1)S(1)}, u32[]{:S(2)}, u32[]{:S(2)}) %all-to-all-start.1) | async-done | bytes 2097184 | tf_op jit(solution)/shard_map/all_to_all | solution.py:39
  94.5 3.2 %all-to-all-start.5 = ((bf16[4,2,2]{1,2,0:T(2,128)(2,1)}), bf16[4,2,2]{1,2,0:T(2,128)(2,1)S(1)}, u32[]{:S(2)}, u32[]{:S(2)}) async-start(bf16[4,2,2]{1,2,0:T(2,128)(2,1)} %copy.59), calls=%async_computation.5 | async-start | bytes 4096 | tf_op jit(solution)/shard_map/all_to_all | solution.py:103
  97.7 1.5 copy.49
  99.2 2.2 all-to-all-done.5
  101.4 3.5 %all-to-all-start.4 = ((bf16[4,2,2,128,128]{4,3,2,1,0:T(8,128)(2,1)}), bf16[4,2,2,128,128]{4,3,2,1,0:T(8,128)(2,1)S(1)}, u32[]{:S(2)}, u32[]{:S(2)}) async-start(bf16[4,2,2,128,128]{4,3,2,1,0:T(8,128)(2,1)} %bitcast.44), calls=%async_computation.4 | async-start | bytes 1048576 | tf_op jit(solution)/shard_map/all_to_all | solution.py:102
  104.9 68.9 %while.11 = (s32[]{:T(128)}, bf16[4,512,4,128]{3,1,0,2:T(8,128)(2,1)}, s32[4]{0:T(128)S(1)}, bf16[2048]{0:T(1024)(128)(2,1)S(1)}, bf16[2048,1]{0,1:T(2,128)(2,1)...) while((s32[]{:T(128)}, ...), condition=%wide.region_3.4_spmd.clone, body=%wide.region_0.3_spmd.clone.sunk | while | flops 2199384576 | bytes 56683728 | solution.py:66
  107.5 4.8 %bitcast_reduce_fusion.3 = (f32[4,512]{1,0:T(4,128)S(1)}, f32[512,4,2048]{2,0,1:T(8,128)S(1)}) fusion(pred[512,2048]{1,0:T(8,128)(4,1)S(1)} %fusion.44, bf16[2048,128]{1,0:T(8,128)(2,1)} %get-tuple-element.186, bf16[2048,4,128]{2,0,1:T(8,128)(2,1)} %get-tuple-element.185, s32[]{:T(128)S(6)} %select_n.39), kind=kOutput, calls=%fused_computation.2.clone.1 | convolution fusion | flops 1086322688 | bytes 18882564 | tf_op jit(solution)/shard_map/while/body/eval_jaxpr/qhe,ke->hqk/dot_general | solution.py:48
  112.2 4.5 %fusion.45 = f32[4,512]{1,0:T(4,128)S(1)} fusion(f32[512,4,2048]{2,0,1:T(8,128)S(1)} %get-tuple-element.152, f32[4,512]{1,0:T(4,128)S(1)} %get-tuple-element.153, pred[512,2048]{1,0:T(8,128)(4,1)S(1)} %fusion.44), kind=kLoop, calls=%fused_computation.5.clone.1 | loop fusion | flops 16775168 | bytes 17842176 | tf_op jit(solution)/shard_map/while/body/eval_jaxpr/reduce_sum | solution.py:57
  116.7 5.4 %fusion.46 = bf16[4,512,4,128]{3,1,0,2:T(8,128)(2,1)} fusion(bf16[4,512,4,128]{3,1,0,2:T(8,128)(2,1)} %get-tuple-element.168, s32[]{:T(128)S(6)} %copy.74, f32[512,4,2048]{2,0,1:T(8,128)S(1)} %get-tuple-element.152, f32[4,512]{1,0:T(4,128)S(1)} %get-tuple-element.153, pred[512,2048]{1,0:T(8,128)(4,1)S(1)} %fusion.44, ...), kind=kOutput, calls=%fused_computation.14.clone.1 | convolution fusion | flops 1091043328 | bytes 18890756 | tf_op jit(solution)/shard_map/while/body/eval_jaxpr/hqk,ke->qhe/dot_general | solution.py:58
  123.5 1.2 fusion.44
  124.7 4.8 %bitcast_reduce_fusion.3 = (f32[4,512]{1,0:T(4,128)S(1)}, f32[512,4,2048]{2,0,1:T(8,128)S(1)}) fusion(pred[512,2048]{1,0:T(8,128)(4,1)S(1)} %fusion.44, bf16[2048,128]{1,0:T(8,128)(2,1)} %get-tuple-element.186, bf16[2048,4,128]{2,0,1:T(8,128)(2,1)} %get-tuple-element.185, s32[]{:T(128)S(6)} %select_n.39), kind=kOutput, calls=%fused_computation.2.clone.1 | convolution fusion | flops 1086322688 | bytes 18882564 | tf_op jit(solution)/shard_map/while/body/eval_jaxpr/qhe,ke->hqk/dot_general | solution.py:48
  129.5 4.5 %fusion.45 = f32[4,512]{1,0:T(4,128)S(1)} fusion(f32[512,4,2048]{2,0,1:T(8,128)S(1)} %get-tuple-element.152, f32[4,512]{1,0:T(4,128)S(1)} %get-tuple-element.153, pred[512,2048]{1,0:T(8,128)(4,1)S(1)} %fusion.44), kind=kLoop, calls=%fused_computation.5.clone.1 | loop fusion | flops 16775168 | bytes 17842176 | tf_op jit(solution)/shard_map/while/body/eval_jaxpr/reduce_sum | solution.py:57
  133.9 5.4 %fusion.46 = bf16[4,512,4,128]{3,1,0,2:T(8,128)(2,1)} fusion(bf16[4,512,4,128]{3,1,0,2:T(8,128)(2,1)} %get-tuple-element.168, s32[]{:T(128)S(6)} %copy.74, f32[512,4,2048]{2,0,1:T(8,128)S(1)} %get-tuple-element.152, f32[4,512]{1,0:T(4,128)S(1)} %get-tuple-element.153, pred[512,2048]{1,0:T(8,128)(4,1)S(1)} %fusion.44, ...), kind=kOutput, calls=%fused_computation.14.clone.1 | convolution fusion | flops 1091043328 | bytes 18890756 | tf_op jit(solution)/shard_map/while/body/eval_jaxpr/hqk,ke->qhe/dot_general | solution.py:58
  141.9 4.8 %bitcast_reduce_fusion.3 = (f32[4,512]{1,0:T(4,128)S(1)}, f32[512,4,2048]{2,0,1:T(8,128)S(1)}) fusion(pred[512,2048]{1,0:T(8,128)(4,1)S(1)} %fusion.44, bf16[2048,128]{1,0:T(8,128)(2,1)} %get-tuple-element.186, bf16[2048,4,128]{2,0,1:T(8,128)(2,1)} %get-tuple-element.185, s32[]{:T(128)S(6)} %select_n.39), kind=kOutput, calls=%fused_computation.2.clone.1 | convolution fusion | flops 1086322688 | bytes 18882564 | tf_op jit(solution)/shard_map/while/body/eval_jaxpr/qhe,ke->hqk/dot_general | solution.py:48
  146.7 4.5 %fusion.45 = f32[4,512]{1,0:T(4,128)S(1)} fusion(f32[512,4,2048]{2,0,1:T(8,128)S(1)} %get-tuple-element.152, f32[4,512]{1,0:T(4,128)S(1)} %get-tuple-element.153, pred[512,2048]{1,0:T(8,128)(4,1)S(1)} %fusion.44), kind=kLoop, calls=%fused_computation.5.clone.1 | loop fusion | flops 16775168 | bytes 17842176 | tf_op jit(solution)/shard_map/while/body/eval_jaxpr/reduce_sum | solution.py:57
  151.2 5.4 %fusion.46 = bf16[4,512,4,128]{3,1,0,2:T(8,128)(2,1)} fusion(bf16[4,512,4,128]{3,1,0,2:T(8,128)(2,1)} %get-tuple-element.168, s32[]{:T(128)S(6)} %copy.74, f32[512,4,2048]{2,0,1:T(8,128)S(1)} %get-tuple-element.152, f32[4,512]{1,0:T(4,128)S(1)} %get-tuple-element.153, pred[512,2048]{1,0:T(8,128)(4,1)S(1)} %fusion.44, ...), kind=kOutput, calls=%fused_computation.14.clone.1 | convolution fusion | flops 1091043328 | bytes 18890756 | tf_op jit(solution)/shard_map/while/body/eval_jaxpr/hqk,ke->qhe/dot_general | solution.py:58
  157.9 1.2 fusion.44
  159.1 4.8 %bitcast_reduce_fusion.3 = (f32[4,512]{1,0:T(4,128)S(1)}, f32[512,4,2048]{2,0,1:T(8,128)S(1)}) fusion(pred[512,2048]{1,0:T(8,128)(4,1)S(1)} %fusion.44, bf16[2048,128]{1,0:T(8,128)(2,1)} %get-tuple-element.186, bf16[2048,4,128]{2,0,1:T(8,128)(2,1)} %get-tuple-element.185, s32[]{:T(128)S(6)} %select_n.39), kind=kOutput, calls=%fused_computation.2.clone.1 | convolution fusion | flops 1086322688 | bytes 18882564 | tf_op jit(solution)/shard_map/while/body/eval_jaxpr/qhe,ke->hqk/dot_general | solution.py:48
  163.9 4.5 %fusion.45 = f32[4,512]{1,0:T(4,128)S(1)} fusion(f32[512,4,2048]{2,0,1:T(8,128)S(1)} %get-tuple-element.152, f32[4,512]{1,0:T(4,128)S(1)} %get-tuple-element.153, pred[512,2048]{1,0:T(8,128)(4,1)S(1)} %fusion.44), kind=kLoop, calls=%fused_computation.5.clone.1 | loop fusion | flops 16775168 | bytes 17842176 | tf_op jit(solution)/shard_map/while/body/eval_jaxpr/reduce_sum | solution.py:57
  168.4 5.4 %fusion.46 = bf16[4,512,4,128]{3,1,0,2:T(8,128)(2,1)} fusion(bf16[4,512,4,128]{3,1,0,2:T(8,128)(2,1)} %get-tuple-element.168, s32[]{:T(128)S(6)} %copy.74, f32[512,4,2048]{2,0,1:T(8,128)S(1)} %get-tuple-element.152, f32[4,512]{1,0:T(4,128)S(1)} %get-tuple-element.153, pred[512,2048]{1,0:T(8,128)(4,1)S(1)} %fusion.44, ...), kind=kOutput, calls=%fused_computation.14.clone.1 | convolution fusion | flops 1091043328 | bytes 18890756 | tf_op jit(solution)/shard_map/while/body/eval_jaxpr/hqk,ke->qhe/dot_general | solution.py:58
  173.8 4.7 %copy.53 = bf16[2048,1,4,128]{3,2,1,0:T(4,128)(2,1)} copy(bf16[2048,1,4,128]{3,0,2,1:T(8,128)(2,1)} %bitcast.120) | data formatting | bytes 4194304 | tf_op jit(solution)/shard_map/reshape | solution.py:67
  178.5 6.0 %all-to-all-start.3 = ((bf16[2048,1,4,128]{3,2,1,0:T(4,128)(2,1)}), bf16[2048,1,4,128]{3,2,1,0:T(4,128)(2,1)S(1)}, u32[]{:S(2)}, u32[]{:S(2)}) async-start(bf16[2048,1,4,128]{3,2,1,0:T(4,128)(2,1)} %copy.53), calls=%async_computation.3 | async-start | bytes 4194304 | tf_op jit(solution)/shard_map/all_to_all | solution.py:68
  185.1 46.0 %all-to-all-done.3 = bf16[2048,1,4,128]{3,2,1,0:T(4,128)(2,1)S(1)} async-done(((bf16[2048,1,4,128]{3,2,1,0:T(4,128)(2,1)}), bf16[2048,1,4,128]{3,2,1,0:T(4,128)(2,1)S(1)}, u32[]{:S(2)}, u32[]{:S(2)}) %all-to-all-start.3) | async-done | bytes 2097184 | tf_op jit(solution)/shard_map/all_to_all | solution.py:68
  231.2 1.6 copy.54
  232.8 2.9 %copy.55 = bf16[256,8,1,4,128]{0,4,3,1,2:T(8,128)(2,1)S(1)} copy(bf16[256,8,1,4,128]{4,0,1,3,2:T(8,128)(2,1)} %bitcast.111) | data formatting | bytes 4194304 | tf_op jit(solution)/shard_map/all_to_all | solution.py:68
  235.6 2.9 %copy.61 = bf16[1,256,4096]{2,1,0:T(8,128)(2,1)} copy(bf16[1,256,4096]{1,2,0:T(8,128)(2,1)S(1)} %bitcast.112) | data formatting | bytes 4194304
  (59 shorter events, 19.3 us)
Async XLA Ops:
  3.1 8.5 %all-to-all-start = ((bf16[8,2,128]{2,1,0:T(2,128)(2,1)}), bf16[8,2,128]{2,1,0:T(2,128)(2,1)S(1)}, u32[]{:S(2)}, u32[]{:S(2)}) async-start(bf16[8,2,128]{2,1,0:T(2,128)(2,1)} %reshape.89), calls=%async_computation | async-start | bytes 8192 | tf_op jit(solution)/shard_map/all_to_all | solution.py:30
  12.8 29.6 %all-to-all-start.2 = ((bf16[256,8,2,128]{3,0,2,1:T(8,128)(2,1)}), bf16[256,8,2,128]{3,0,2,1:T(8,128)(2,1)S(1)}, u32[]{:S(2)}, u32[]{:S(2)}) async-start(bf16[256,8,2,128]{3,0,2,1:T(8,128)(2,1)} %bitcast.6), calls=%async_computation.2 | async-start | bytes 2097152 | tf_op jit(solution)/shard_map/all_to_all | solution.py:29
  23.5 25.1 %copy-start = (bf16[1,256,512]{2,1,0:T(8,128)(2,1)S(1)}, bf16[1,256,512]{2,1,0:T(8,128)(2,1)}, u32[]{:S(2)}) copy-start(bf16[1,256,512]{2,1,0:T(8,128)(2,1)} %param.9) | copy-start | bytes 786436
  25.9 26.0 %copy-start.1 = (s32[1,8,1]{1,2,0:T(1,128)S(1)}, s32[1,8,1]{1,2,0:T(1,128)}, u32[]{:S(2)}) copy-start(s32[1,8,1]{1,2,0:T(1,128)} %param.11) | copy-start | bytes 100
  42.4 52.1 %all-to-all-start.1 = ((bf16[256,8,4,128]{3,0,2,1:T(8,128)(2,1)}), bf16[256,8,4,128]{3,0,2,1:T(8,128)(2,1)S(1)}, u32[]{:S(2)}, u32[]{:S(2)}) async-start(bf16[256,8,4,128]{3,0,2,1:T(8,128)(2,1)} %copy.48), calls=%async_computation.1 | async-start | bytes 4194304 | tf_op jit(solution)/shard_map/all_to_all | solution.py:39
  94.5 6.9 %all-to-all-start.5 = ((bf16[4,2,2]{1,2,0:T(2,128)(2,1)}), bf16[4,2,2]{1,2,0:T(2,128)(2,1)S(1)}, u32[]{:S(2)}, u32[]{:S(2)}) async-start(bf16[4,2,2]{1,2,0:T(2,128)(2,1)} %copy.59), calls=%async_computation.5 | async-start | bytes 4096 | tf_op jit(solution)/shard_map/all_to_all | solution.py:103
  101.4 77.1 %all-to-all-start.4 = ((bf16[4,2,2,128,128]{4,3,2,1,0:T(8,128)(2,1)}), bf16[4,2,2,128,128]{4,3,2,1,0:T(8,128)(2,1)S(1)}, u32[]{:S(2)}, u32[]{:S(2)}) async-start(bf16[4,2,2,128,128]{4,3,2,1,0:T(8,128)(2,1)} %bitcast.44), calls=%async_computation.4 | async-start | bytes 1048576 | tf_op jit(solution)/shard_map/all_to_all | solution.py:102
  178.5 52.6 %all-to-all-start.3 = ((bf16[2048,1,4,128]{3,2,1,0:T(4,128)(2,1)}), bf16[2048,1,4,128]{3,2,1,0:T(4,128)(2,1)S(1)}, u32[]{:S(2)}, u32[]{:S(2)}) async-start(bf16[2048,1,4,128]{3,2,1,0:T(4,128)(2,1)} %copy.53), calls=%async_computation.3 | async-start | bytes 4194304 | tf_op jit(solution)/shard_map/all_to_all | solution.py:68
where the time goes:
time: 244 us; the launch traced here: 239 us
  waiting for transfers between devices  104 us (43%)
  matrix products  41.3 us (17%)
  local copies, waits for them, and re-layouts  33.1 us (14%)
  starting transfers between devices  32.2 us (13%)
  other arithmetic  25.2 us (10%)
  loops' own time  2.64 us (1%)
    all_to_all x1, waiting for transfers between devices, split_heads(): lax.all_to_all(result, 'ctx', split_axis=0, concat_axis=1, tiled=True)  46 us
    all_to_all x1, waiting for transfers between devices, split_heads(): lax.all_to_all(shaped, 'ctx', split_axis=1, concat_axis=0, tiled=True)[:, 0]  39.3 us
    dot_general x4, matrix products, one_block(): jnp.einsum('hqk,ke->qhe', weights.astype(jnp.bfloat16), value_all, prefer...  21.7 us
    dot_general x4, matrix products, one_block(): jnp.einsum('qhe,ke->hqk', query_block, key_all, preferred_element_type=jn...  19 us
    reduce_sum x4, other arithmetic, one_block(): totals = jnp.sum(weights, axis=-1)  17.9 us
    all_to_all x1, waiting for transfers between devices, split_heads(): lax.all_to_all(spread, 'ctx', split_axis=1, concat_axis=0, tiled=True)  16.5 us
    unnamed x13, local copies, waits for them, and re-layouts  8.96 us
    all_to_all x1, starting transfers between devices, split_heads(): lax.all_to_all(spread, 'ctx', split_axis=1, concat_axis=0, tiled=True)  7.41 us
  transfers between devices with their start and end apart: 6, of which 4 were waited for; matrix products, arithmetic and copies ran while one was open for 37% of the time, Pallas kernels for 0%

commit v1 on v0

v1 whole, which is shorter than its diff:
```python
import functools
import math

import jax
import jax.numpy as jnp
from jax import lax
from jax.experimental import pallas as pl
from jax.experimental.pallas import tpu as pltpu
from jax.sharding import PartitionSpec as P

E = 128
PAGE = 128
DOC_ROWS = 16
epsilon = 1e-06
hidden_score = -1e30
MESH = pl.DeviceIdType.MESH


def window_blocks(length, tokens):
    longest = length * 5 // 8
    return min(length // tokens - 1, (longest - 1 + tokens - 1) // tokens)


def kernel(
    heads, key_heads, ctx_count, groups_n, window, depth,
    query_ref, key_ref, value_ref, doc_ref, owner_ref,
    out_ref, pool_ref, scale_ref,
    kv, query, result, key_aug, value_aug, query_mask, key_mask, causal, packed, packed_scales,
    local_sem, query_sem, out_sem, up_sem, side_sem, recv_sem,
    page_sem, page_recv, scale_sem, scale_recv, page_local,
):
    tokens = query.shape[0]
    per_key = heads // key_heads
    group = lax.axis_index("group")
    ctx = lax.axis_index("ctx")
    column = lax.rem(ctx, 2)
    partner = ctx + 1 - 2 * column
    passed = [k for k in range(2, window + 2, 2)]
    body = 2 * tokens + DOC_ROWS
    length = (window + 1) * tokens

    locals_ = []
    for h in range(key_heads):
        cols = pl.ds(h * E, E)
        locals_.append(pltpu.make_async_copy(key_ref.at[0, :, cols], kv.at[0, h, pl.ds(0, tokens)], local_sem.at[3 * h]))
        locals_.append(pltpu.make_async_copy(value_ref.at[0, :, cols], kv.at[0, h, pl.ds(tokens, tokens)], local_sem.at[3 * h + 1]))
        locals_.append(pltpu.make_async_copy(doc_ref, kv.at[0, h, pl.ds(2 * tokens, DOC_ROWS)], local_sem.at[3 * h + 2]))
    for copy in locals_:
        copy.start()
    query_copy = pltpu.make_async_copy(query_ref.at[0], query, query_sem)
    query_copy.start()

    barrier = pltpu.get_barrier_semaphore()
    for step in range(1, groups_n):
        pl.semaphore_signal(barrier, inc=1, device_id=(lax.rem(group + step, groups_n), ctx), device_id_type=MESH)
    pl.semaphore_signal(barrier, inc=1, device_id=(group, partner), device_id_type=MESH)

    @pl.when(ctx >= 2)
    def _():
        pl.semaphore_signal(barrier, inc=1, device_id=(group, ctx - 2), device_id_type=MESH)

    @pl.when(ctx + 2 < ctx_count)
    def _():
        pl.semaphore_signal(barrier, inc=1, device_id=(group, ctx + 2), device_id_type=MESH)

    greeted = groups_n + jnp.where(ctx >= 2, 1, 0) + jnp.where(ctx + 2 < ctx_count, 1, 0)
    pl.semaphore_wait(barrier, greeted)

    for copy in locals_:
        copy.wait()

    def up_copy(k, h):
        return pltpu.make_async_remote_copy(
            kv.at[k, h], kv.at[k + 2, h], up_sem.at[k, h], recv_sem.at[k + 2, h],
            device_id=(group, ctx + 2), device_id_type=MESH)

    def side_copy(k, h, there):
        return pltpu.make_async_remote_copy(
            kv.at[k, h], kv.at[there, h], side_sem.at[k, h], recv_sem.at[there, h],
            device_id=(group, partner), device_id_type=MESH)

    def each_send(k, h, act):
        here = ctx >= k
        limits = (k + 2 <= window, k + 2 <= window + 1)
        if limits[1]:
            ok = here & (ctx + 2 < ctx_count)
            if not limits[0]:
                ok = ok & (column == 1)

            @pl.when(ok)
            def _():
                act(up_copy(k, h))

        if k + 1 <= window:
            @pl.when(here & (column == 0))
            def _():
                act(side_copy(k, h, k + 1))

        if k >= 2 and k - 1 <= window:
            @pl.when(here & (column == 1))
            def _():
                act(side_copy(k, h, k - 1))

    def arrives(k):
        ok = ctx >= k
        return ok & (column == 1) if k > window else ok

    def await_block(k, h):
        pltpu.make_async_remote_copy(
            kv.at[k, h], kv.at[k, h], up_sem.at[k, h], recv_sem.at[k, h],
            device_id=(group, partner), device_id_type=MESH).wait_recv()

    def pass_on(k, h):
        @pl.when(arrives(k))
        def _():
            await_block(k, h)

        each_send(k, h, lambda copy: copy.start())

    ahead = min(2, key_heads)
    for h in range(ahead):
        each_send(0, h, lambda copy: copy.start())

    for k in range(1, window + 1):
        @pl.when(ctx < k)
        def _(k=k):
            kv[k] = jnp.zeros(kv.shape[1:], kv.dtype)
            kv[k, 0, pl.ds(2 * tokens, DOC_ROWS), :] = jnp.full((DOC_ROWS, E), -1.0, kv.dtype)

    rows = lax.broadcasted_iota(jnp.int32, (tokens, tokens), 0)
    cols = lax.broadcasted_iota(jnp.int32, (tokens, tokens), 1)
    causal[...] = jnp.where(rows >= cols, 0.0, hidden_score)
    lanes = lax.broadcasted_iota(jnp.int32, (E, E), 1).astype(jnp.float32)

    def mark_columns(k, b):
        line = kv[k, 0, pl.ds(2 * tokens, DOC_ROWS), :].astype(jnp.float32)[b:b + 1, :]
        return jnp.transpose(jnp.broadcast_to(line, (E, E)))

    for b in range(tokens // E):
        query_mask[pl.ds(b * E, E), :] = jnp.where(mark_columns(0, b) == lanes, 1.0, 0.0).astype(jnp.bfloat16)

    blocks_n = tokens // PAGE
    page_count = blocks_n * key_heads
    owner = [owner_ref[p] for p in range(page_count)]
    rank = []
    for p in range(page_count):
        r = jnp.int32(0)
        for e in range(p):
            r = r + jnp.where(owner[e] == owner[p], 1, 0)
        rank.append(r)
    line_of = lax.broadcasted_iota(jnp.int32, (8, E), 0)
    for part in range(2):
        for p in range(page_count):
            b, h = p // key_heads, p % key_heads
            page = kv[0, h, pl.ds(part * tokens + b * PAGE, PAGE), :].astype(jnp.float32)
            scale = (jnp.max(jnp.max(jnp.abs(page), axis=0, keepdims=True), axis=1, keepdims=True) + epsilon)
            scale = scale.astype(jnp.bfloat16).astype(jnp.float32)
            stored = (page / scale).astype(jnp.bfloat16).astype(jnp.float32)
            for o in range(groups_n):
                for r in range(depth):
                    chosen = jnp.where((owner[p] == o) & (rank[p] == r), 1.0, 0.0)
                    term = (stored * chosen).astype(jnp.bfloat16)
                    spread = jnp.where(line_of == 2 * r + part, scale * chosen, 0.0)
                    if p == 0:
                        packed[o, r, part] = term
                    else:
                        packed[o, r, part] += term
                    if p == 0 and part == 0 and r == 0:
                        packed_scales[o] = spread
                    else:
                        packed_scales[o] += spread

    for h in range(ahead):
        for k in passed:
            pass_on(k, h)

    def page_copies(step, act):
        to = lax.rem(group + step, groups_n)
        act(pltpu.make_async_remote_copy(
            packed.at[to], pool_ref.at[0, pl.ds(group * depth, depth)], page_sem.at[step], page_recv.at[step],
            device_id=(to, ctx), device_id_type=MESH))
        act(pltpu.make_async_remote_copy(
            packed_scales.at[to], scale_ref.at[group], scale_sem.at[step], scale_recv.at[step],
            device_id=(to, ctx), device_id_type=MESH))

    own_page = pltpu.make_async_copy(packed.at[group], pool_ref.at[0, pl.ds(group * depth, depth)], page_local.at[0])
    own_scale = pltpu.make_async_copy(packed_scales.at[group], scale_ref.at[group], page_local.at[1])

    query_copy.wait()
    factor = math.log2(math.e) / math.sqrt(E)
    pair = 2
    inner = per_key // pair

    def out_copy(h):
        wide = pl.ds(h * per_key * E, per_key * E)
        return pltpu.make_async_copy(result.at[:, wide], out_ref.at[0, :, wide], out_sem.at[h])

    for h in range(key_heads):
        if h + ahead < key_heads:
            each_send(0, h + ahead, lambda copy: copy.start())
        for k in range(1, window + 1):
            if k % 2 == 1:
                @pl.when(ctx >= k)
                def _(k=k):
                    await_block(k, h)
        if h == 0:
            for k in range(window + 1):
                for b in range(tokens // E):
                    key_mask[pl.ds(k * tokens + b * E, E), :] = jnp.where(
                        mark_columns(k, b) == lanes, 0.0, hidden_score).astype(jnp.bfloat16)
            key_aug[:, pl.ds(E, E)] = key_mask[...]
            value_aug[:, pl.ds(E, E)] = jnp.ones((length, E), jnp.bfloat16)
        for k in range(window + 1):
            key_aug[pl.ds(k * tokens, tokens), pl.ds(0, E)] = kv[k, h, pl.ds(0, tokens), :]
            value_aug[pl.ds(k * tokens, tokens), pl.ds(0, E)] = kv[k, h, pl.ds(tokens, tokens), :]

        def one_pair(i, carry):
            if h + ahead < key_heads:
                for n, k in enumerate(passed):
                    @pl.when(i == n % inner)
                    def _(k=k):
                        pass_on(k, h + ahead)
            for j in range(pair):
                at = pl.ds(pl.multiple_of((h * per_key + i * pair + j) * E, E), E)
                wide = jnp.concatenate([query[:, at], query_mask[...]], axis=1)
                scores = lax.dot_general(wide, key_aug[...], (((1,), (1,)), ((), ())),
                                         preferred_element_type=jnp.float32)
                near = scores[:, :tokens] + causal[...]
                far = scores[:, tokens:]
                largest = jnp.maximum(jnp.max(near, axis=1, keepdims=True), jnp.max(far, axis=1, keepdims=True))
                weights = jnp.concatenate(
                    [jnp.exp2((near - largest) * factor).astype(jnp.bfloat16),
                     jnp.exp2((far - largest) * factor).astype(jnp.bfloat16)], axis=1)
                summed = jnp.dot(weights, value_aug[...], preferred_element_type=jnp.float32)
                result[:, at] = (summed[:, :E] / summed[:, E:]).astype(jnp.bfloat16)
            return carry

        lax.fori_loop(0, inner, one_pair, 0)
        out_copy(h).start()
        if h == 0:
            own_page.start()
            own_scale.start()
            for step in range(1, groups_n):
                page_copies(step, lambda copy: copy.start())

    for h in range(key_heads):
        for k in [0] + passed:
            each_send(k, h, lambda copy: copy.wait_send())
    for step in range(1, groups_n):
        page_copies(step, lambda copy: copy.wait())
    own_page.wait()
    own_scale.wait()
    for h in range(key_heads):
        out_copy(h).wait()


def local(query_rows, key_rows, value_rows, documents, owners):
    tokens = query_rows.shape[1]
    heads = query_rows.shape[2] // E
    key_heads = key_rows.shape[2] // E
    ctx_count = lax.axis_size("ctx")
    groups_n = lax.axis_size("group")
    window = window_blocks(tokens * ctx_count, tokens)
    page_count = owners.shape[1]
    depth = max(2, (page_count + groups_n - 1) // groups_n)
    marks = documents[0].astype(jnp.bfloat16).reshape(tokens // E, E)
    marks = jnp.pad(marks, ((0, DOC_ROWS - tokens // E), (0, 0)))
    slots = window + 2
    length = (window + 1) * tokens
    anywhere = pl.BlockSpec(memory_space=pl.ANY)
    attended, pool, scales = pl.pallas_call(
        functools.partial(kernel, heads, key_heads, ctx_count, groups_n, window, depth),
        out_shape=(
            jax.ShapeDtypeStruct(query_rows.shape, jnp.bfloat16),
            jax.ShapeDtypeStruct((1, groups_n * depth, 2, PAGE, E), jnp.bfloat16),
            jax.ShapeDtypeStruct((groups_n, 8, E), jnp.float32),
        ),
        in_specs=[anywhere] * 4 + [pl.BlockSpec(memory_space=pltpu.SMEM)],
        out_specs=(anywhere, anywhere, anywhere),
        scratch_shapes=[
            pltpu.VMEM((slots, key_heads, 2 * tokens + DOC_ROWS, E), jnp.bfloat16),
            pltpu.VMEM((tokens, heads * E), jnp.bfloat16),
            pltpu.VMEM((tokens, heads * E), jnp.bfloat16),
            pltpu.VMEM((length, 2 * E), jnp.bfloat16),
            pltpu.VMEM((length, 2 * E), jnp.bfloat16),
            pltpu.VMEM((tokens, E), jnp.bfloat16),
            pltpu.VMEM((length, E), jnp.bfloat16),
            pltpu.VMEM((tokens, tokens), jnp.float32),
            pltpu.VMEM((groups_n, depth, 2, PAGE, E), jnp.bfloat16),
            pltpu.VMEM((groups_n, 8, E), jnp.float32),
            pltpu.SemaphoreType.DMA((3 * key_heads,)),
            pltpu.SemaphoreType.DMA,
            pltpu.SemaphoreType.DMA((key_heads,)),
            pltpu.SemaphoreType.DMA((slots, key_heads)),
            pltpu.SemaphoreType.DMA((slots, key_heads)),
            pltpu.SemaphoreType.DMA((slots, key_heads)),
            pltpu.SemaphoreType.DMA((groups_n,)),
            pltpu.SemaphoreType.DMA((groups_n,)),
            pltpu.SemaphoreType.DMA((groups_n,)),
            pltpu.SemaphoreType.DMA((groups_n,)),
            pltpu.SemaphoreType.DMA((2,)),
        ],
        compiler_params=pltpu.CompilerParams(
            collective_id=0, has_side_effects=True, vmem_limit_bytes=56 * 1024 * 1024),
        name="attend_and_deliver",
    )(query_rows, key_rows, value_rows, marks, owners[0, :, 0])
    page_scales = scales[:, : 2 * depth, 0].reshape(1, groups_n * depth, 2).astype(jnp.bfloat16)
    return (attended, pool, page_scales)


def solution(mesh):
    placed = (
        P("group", "ctx", None),
        P("group", "ctx", None),
        P("group", "ctx", None),
        P("group", "ctx"),
        P("group", "ctx", None),
    )
    return jax.shard_map(
        local,
        mesh=mesh,
        in_specs=placed,
        out_specs=(
            P("group", "ctx", None),
            P("group", "ctx", None, None, None),
            P("group", "ctx", None),
        ),
        check_vma=False,
    )
```

time: 244 us -> 65.2 us (0.27); the launches traced: 239 us -> 64.9 us
  waiting for transfers between devices: 104 us -> 0 us
  Pallas kernels: 0 us -> 57.5 us
  matrix products: 41.3 us -> 0 us
  starting transfers between devices: 32.2 us -> 0 us
  local copies, waits for them, and re-layouts: 33.1 us -> 6.08 us
  other arithmetic: 25.2 us -> 0.7 us
  loops' own time: 2.64 us -> 0 us
    all_to_all x6 -> x0, waiting for transfers between devices: 104 us -> none  [the longest x1 46 us: split_heads(): lax.all_to_all(result, 'ctx', split_axis=0, concat_axis=1, tiled=True)]
    pallas_call x0 -> x1, Pallas kernels: none -> 57.5 us  [local(): pl.pallas_call(functools.partial(kernel, heads, key_heads, ctx_count, gro...]
    dot_general x10 -> x0, matrix products: 41.3 us -> none  [the longest x4 21.7 us: one_block(): jnp.einsum('hqk,ke->qhe', weights.astype(jnp.bfloat16), value_all, prefer...]
    all_to_all x6 -> x0, starting transfers between devices: 32.2 us -> none  [the longest x1 7.41 us: split_heads(): lax.all_to_all(spread, 'ctx', split_axis=1, concat_axis=0, tiled=True)]
    reduce_sum x5 -> x0, other arithmetic: 18.1 us -> none  [the longest x4 17.9 us: one_block(): totals = jnp.sum(weights, axis=-1)]
    another operation x6 -> x0, local copies, waits for them, and re-layouts: 6.27 us -> none  [the longest x1 2.39 us: split_heads(): shaped = queries_here.reshape(tokens, ctx_count, per_device, E)]
    all_to_all x6 -> x0, local copies, waits for them, and re-layouts: 6.07 us -> none  [the longest x2 4.45 us: split_heads(): lax.all_to_all(result, 'ctx', split_axis=0, concat_axis=1, tiled=True)]
    reshape x4 -> x0, local copies, waits for them, and re-layouts: 5.98 us -> none  [the longest x1 4.71 us: split_heads(): result = blocks.reshape(length, 1, head_count, E)]
  transfers between devices with their start and end apart: 6 -> 0, of which waited for: 4 -> 0; matrix products, arithmetic and copies ran while one was open for 37% -> 0% of each run, Pallas kernels for 0% -> 0%
where the time goes in v1:
time: 65.2 us; the launch traced here: 64.9 us
  Pallas kernels  57.5 us (88%)
  local copies, waits for them, and re-layouts  6.08 us (9%)
  other arithmetic  0.7 us (1%)
    pallas_call x1, Pallas kernels, local(): pl.pallas_call(functools.partial(kernel, heads, key_heads, ctx_count, gro...  57.5 us
    unnamed x5, local copies, waits for them, and re-layouts  4.59 us

profile of v1, /device:TPU:28, one launch (start us, length us, event | category | flops | bytes accessed | tf_op | source)
XLA Modules:
  0.0 64.9 jit_solution(11753034555731068436)
XLA Ops:
  0.6 0.7 %convert_reduce_fusion = bf16[256]{0:T(256)(128)(2,1)S(1)} fusion(s32[1,256]{1,0:T(1,128)} %param.8), kind=kLoop, calls=%fused_computation.2 | loop fusion | flops 256 | bytes 1536 | tf_op jit(solution)/shard_map/convert_element_type | solution.py:266
  1.3 0.6 pad.4.doc_ref
  1.9 57.5 %attend_and_deliver.1 = (bf16[1,256,4096]{2,1,0:T(8,128)(2,1)}, bf16[1,8,2,128,128]{4,3,2,1,0:T(8,128)(2,1)}, f32[4,8,128]{2,1,0:T(8,128)}) custom-call(bf16[1,256,4096]{2,1,0:T(8,128)(2,1)} %query_ref.1, bf16[1,256,512]{2,1,0:T(8,128)(2,1)} %key_ref.1, bf16[1,256,512]{2,1,0:T(8,128)(2,1)} %value_ref.1, bf16[16,128]{1,0:T(8,128)(2,1)} %pad.4.doc_ref, s32[8]{0:T(128)} %bitcast.3), custom_call_target="tpu_custom_call" | custom-call | tf_op jit(solution)/shard_map/attend_and_deliver/pallas_call | solution.py:271
  59.4 0.8 %fusion = bf16[4,4]{1,0:T(4,128)(2,1)S(1)} fusion(f32[4,8,128]{2,1,0:T(8,128)} %get-tuple-element.8), kind=kLoop, calls=%fused_computation.1 | loop fusion | bytes 64 | tf_op jit(solution)/shard_map/slice | solution.py:307
  60.2 0.1 convert_element_type.23
  60.3 0.6 copy.9
  60.9 0.0 copy-start
  60.9 3.2 %copy.12 = bf16[1,256,4096]{2,1,0:T(8,128)(2,1)} copy(bf16[1,256,4096]{2,1,0:T(8,128)(2,1)} %get-tuple-element.18) | data formatting | bytes 4194304
  64.1 0.0 copy-done
  64.1 0.8 %copy.13 = bf16[1,8,2,128,128]{4,3,2,1,0:T(8,128)(2,1)} copy(bf16[1,8,2,128,128]{4,3,2,1,0:T(8,128)(2,1)S(1)} %copy-done) | data formatting | bytes 1048576
Async XLA Ops:
  60.9 3.2 %copy-start = (bf16[1,8,2,128,128]{4,3,2,1,0:T(8,128)(2,1)S(1)}, bf16[1,8,2,128,128]{4,3,2,1,0:T(8,128)(2,1)}, u32[]{:S(2)}) copy-start(bf16[1,8,2,128,128]{4,3,2,1,0:T(8,128)(2,1)} %get-tuple-element.19) | copy-start | bytes 1572868

commit v2 on v1

--- a/solution.py
+++ b/solution.py
@@ -25,7 +25,7 @@
     heads, key_heads, ctx_count, groups_n, window, depth,
     query_ref, key_ref, value_ref, doc_ref, owner_ref,
     out_ref, pool_ref, scale_ref,
-    kv, query, result, key_aug, value_aug, query_mask, key_mask, causal, packed, packed_scales,
+    kv, marks, query, result, key_aug, value_aug, query_mask, key_mask, causal, packed, packed_scales,
     local_sem, query_sem, out_sem, up_sem, side_sem, recv_sem,
     page_sem, page_recv, scale_sem, scale_recv, page_local,
 ):
@@ -35,16 +35,30 @@
     ctx = lax.axis_index("ctx")
     column = lax.rem(ctx, 2)
     partner = ctx + 1 - 2 * column
-    passed = [k for k in range(2, window + 2, 2)]
-    body = 2 * tokens + DOC_ROWS
+    turn = window - 2 if window % 2 == 1 and window >= 3 else 0
+    evens = [k for k in range(2, window + 1, 2)]
+
+    def climbs(col, h):
+        return False
+
+    def passed(h):
+        late = [turn] if climbs(0, h) or climbs(1, h) else []
+        return evens + late + ([window + 1] if window % 2 == 1 and not climbs(0, h) else [])
+
+    def chunk(k, h):
+        return kv.at[k, h, pl.ds(0, 2 * tokens + (DOC_ROWS if h == 0 else 0))]
+
     length = (window + 1) * tokens
+
+    marks[...] = jnp.zeros(marks.shape, marks.dtype)
+    for b in range(tokens // E):
+        marks[b:b + 1, :] = doc_ref[:, b * E:(b + 1) * E].astype(jnp.float32).astype(jnp.bfloat16)
 
     locals_ = []
     for h in range(key_heads):
         cols = pl.ds(h * E, E)
-        locals_.append(pltpu.make_async_copy(key_ref.at[0, :, cols], kv.at[0, h, pl.ds(0, tokens)], local_sem.at[3 * h]))
-        locals_.append(pltpu.make_async_copy(value_ref.at[0, :, cols], kv.at[0, h, pl.ds(tokens, tokens)], local_sem.at[3 * h + 1]))
-        locals_.append(pltpu.make_async_copy(doc_ref, kv.at[0, h, pl.ds(2 * tokens, DOC_ROWS)], local_sem.at[3 * h + 2]))
+        locals_.append(pltpu.make_async_copy(key_ref.at[0, :, cols], kv.at[0, h, pl.ds(0, tokens)], local_sem.at[2 * h]))
+        locals_.append(pltpu.make_async_copy(value_ref.at[0, :, cols], kv.at[0, h, pl.ds(tokens, tokens)], local_sem.at[2 * h + 1]))
     for copy in locals_:
         copy.start()
     query_copy = pltpu.make_async_copy(query_ref.at[0], query, query_sem)
@@ -65,38 +79,46 @@
 
     greeted = groups_n + jnp.where(ctx >= 2, 1, 0) + jnp.where(ctx + 2 < ctx_count, 1, 0)
     pl.semaphore_wait(barrier, greeted)
+    mark_copy = pltpu.make_async_copy(marks, kv.at[0, 0, pl.ds(2 * tokens, DOC_ROWS)], local_sem.at[2 * key_heads])
+    mark_copy.start()
+    mark_copy.wait()
 
     for copy in locals_:
         copy.wait()
 
     def up_copy(k, h):
         return pltpu.make_async_remote_copy(
-            kv.at[k, h], kv.at[k + 2, h], up_sem.at[k, h], recv_sem.at[k + 2, h],
+            chunk(k, h), chunk(k + 2, h), up_sem.at[k, h], recv_sem.at[k + 2, h],
             device_id=(group, ctx + 2), device_id_type=MESH)
 
     def side_copy(k, h, there):
         return pltpu.make_async_remote_copy(
-            kv.at[k, h], kv.at[there, h], side_sem.at[k, h], recv_sem.at[there, h],
+            chunk(k, h), chunk(there, h), side_sem.at[k, h], recv_sem.at[there, h],
             device_id=(group, partner), device_id_type=MESH)
 
     def each_send(k, h, act):
         here = ctx >= k
-        limits = (k + 2 <= window, k + 2 <= window + 1)
-        if limits[1]:
-            ok = here & (ctx + 2 < ctx_count)
-            if not limits[0]:
-                ok = ok & (column == 1)
-
-            @pl.when(ok)
+        above = here & (ctx + 2 < ctx_count)
+        if k % 2 == 1:
+            pick = [col for col in range(2) if climbs(col, h)]
+            up = above if len(pick) == 2 else above & (column == pick[0])
+        elif k + 2 <= window:
+            up = above
+        elif k + 2 == window + 1 and not climbs(0, h):
+            up = above & (column == 1)
+        else:
+            up = None
+        if up is not None:
+            @pl.when(up)
             def _():
                 act(up_copy(k, h))
 
-        if k + 1 <= window:
+        if k % 2 == 0 and k + 1 <= window and not (k + 1 == window and climbs(1, h)):
             @pl.when(here & (column == 0))
             def _():
                 act(side_copy(k, h, k + 1))
 
-        if k >= 2 and k - 1 <= window:
+        if k % 2 == 0 and k >= 2:
             @pl.when(here & (column == 1))
             def _():
                 act(side_copy(k, h, k - 1))
@@ -107,7 +129,7 @@
 
     def await_block(k, h):
         pltpu.make_async_remote_copy(
-            kv.at[k, h], kv.at[k, h], up_sem.at[k, h], recv_sem.at[k, h],
+            chunk(k, h), chunk(k, h), up_sem.at[k, h], recv_sem.at[k, h],
             device_id=(group, partner), device_id_type=MESH).wait_recv()
 
     def pass_on(k, h):
@@ -117,8 +139,9 @@
 
         each_send(k, h, lambda copy: copy.start())
 
-    ahead = min(2, key_heads)
-    for h in range(ahead):
+    ahead = min(1, key_heads)
+    own_ahead = min(2, key_heads)
+    for h in range(own_ahead):
         each_send(0, h, lambda copy: copy.start())
 
     for k in range(1, window + 1):
@@ -139,40 +162,41 @@
     for b in range(tokens // E):
         query_mask[pl.ds(b * E, E), :] = jnp.where(mark_columns(0, b) == lanes, 1.0, 0.0).astype(jnp.bfloat16)
 
-    blocks_n = tokens // PAGE
-    page_count = blocks_n * key_heads
-    owner = [owner_ref[p] for p in range(page_count)]
-    rank = []
-    for p in range(page_count):
-        r = jnp.int32(0)
-        for e in range(p):
-            r = r + jnp.where(owner[e] == owner[p], 1, 0)
-        rank.append(r)
-    line_of = lax.broadcasted_iota(jnp.int32, (8, E), 0)
-    for part in range(2):
+    for h in range(ahead):
+        for k in passed(h):
+            pass_on(k, h)
+
+    def pack_pages():
+        blocks_n = tokens // PAGE
+        page_count = blocks_n * key_heads
+        owner = [owner_ref[p] for p in range(page_count)]
+        rank = []
         for p in range(page_count):
-            b, h = p // key_heads, p % key_heads
-            page = kv[0, h, pl.ds(part * tokens + b * PAGE, PAGE), :].astype(jnp.float32)
-            scale = (jnp.max(jnp.max(jnp.abs(page), axis=0, keepdims=True), axis=1, keepdims=True) + epsilon)
-            scale = scale.astype(jnp.bfloat16).astype(jnp.float32)
-            stored = (page / scale).astype(jnp.bfloat16).astype(jnp.float32)
-            for o in range(groups_n):
-                for r in range(depth):
-                    chosen = jnp.where((owner[p] == o) & (rank[p] == r), 1.0, 0.0)
-                    term = (stored * chosen).astype(jnp.bfloat16)
-                    spread = jnp.where(line_of == 2 * r + part, scale * chosen, 0.0)
-                    if p == 0:
-                        packed[o, r, part] = term
-                    else:
-                        packed[o, r, part] += term
-                    if p == 0 and part == 0 and r == 0:
-                        packed_scales[o] = spread
-                    else:
-                        packed_scales[o] += spread
-
-    for h in range(ahead):
-        for k in passed:
-            pass_on(k, h)
+            r = jnp.int32(0)
+            for e in range(p):
+                r = r + jnp.where(owner[e] == owner[p], 1, 0)
+            rank.append(r)
+        line_of = lax.broadcasted_iota(jnp.int32, (8, E), 0)
+        for part in range(2):
+            for p in range(page_count):
+                b, h = p // key_heads, p % key_heads
+                page = kv[0, h, pl.ds(part * tokens + b * PAGE, PAGE), :].astype(jnp.float32)
+                scale = (jnp.max(jnp.max(jnp.abs(page), axis=0, keepdims=True), axis=1, keepdims=True) + epsilon)
+                scale = scale.astype(jnp.bfloat16).astype(jnp.float32)
+                stored = (page / scale).astype(jnp.bfloat16).astype(jnp.float32)
+                for o in range(groups_n):
+                    for r in range(depth):
+                        chosen = jnp.where((owner[p] == o) & (rank[p] == r), 1.0, 0.0)
+                        term = (stored * chosen).astype(jnp.bfloat16)
+                        spread = jnp.where(line_of == 2 * r + part, scale * chosen, 0.0)
+                        if p == 0:
+                            packed[o, r, part] = term
+                        else:
+                            packed[o, r, part] += term
+                        if p == 0 and part == 0 and r == 0:
+                            packed_scales[o] = spread
+                        else:
+                            packed_scales[o] += spread
 
     def page_copies(step, act):
         to = lax.rem(group + step, groups_n)
@@ -196,10 +220,10 @@
         return pltpu.make_async_copy(result.at[:, wide], out_ref.at[0, :, wide], out_sem.at[h])
 
     for h in range(key_heads):
-        if h + ahead < key_heads:
-            each_send(0, h + ahead, lambda copy: copy.start())
+        if h + own_ahead < key_heads:
+            each_send(0, h + own_ahead, lambda copy: copy.start())
         for k in range(1, window + 1):
-            if k % 2 == 1:
+            if k not in passed(h):
                 @pl.when(ctx >= k)
                 def _(k=k):
                     await_block(k, h)
@@ -216,7 +240,7 @@
 
         def one_pair(i, carry):
             if h + ahead < key_heads:
-                for n, k in enumerate(passed):
+                for n, k in enumerate(passed(h + ahead)):
                     @pl.when(i == n % inner)
                     def _(k=k):
                         pass_on(k, h + ahead)
@@ -238,13 +262,15 @@
         lax.fori_loop(0, inner, one_pair, 0)
         out_copy(h).start()
         if h == 0:
+            pack_pages()
+        if h == min(1, key_heads - 1):
             own_page.start()
             own_scale.start()
             for step in range(1, groups_n):
                 page_copies(step, lambda copy: copy.start())
 
     for h in range(key_heads):
-        for k in [0] + passed:
+        for k in [0] + passed(h):
             each_send(k, h, lambda copy: copy.wait_send())
     for step in range(1, groups_n):
         page_copies(step, lambda copy: copy.wait())
@@ -263,8 +289,6 @@
     window = window_blocks(tokens * ctx_count, tokens)
     page_count = owners.shape[1]
     depth = max(2, (page_count + groups_n - 1) // groups_n)
-    marks = documents[0].astype(jnp.bfloat16).reshape(tokens // E, E)
-    marks = jnp.pad(marks, ((0, DOC_ROWS - tokens // E), (0, 0)))
     slots = window + 2
     length = (window + 1) * tokens
     anywhere = pl.BlockSpec(memory_space=pl.ANY)
@@ -275,10 +299,11 @@
             jax.ShapeDtypeStruct((1, groups_n * depth, 2, PAGE, E), jnp.bfloat16),
             jax.ShapeDtypeStruct((groups_n, 8, E), jnp.float32),
         ),
-        in_specs=[anywhere] * 4 + [pl.BlockSpec(memory_space=pltpu.SMEM)],
+        in_specs=[anywhere] * 3 + [pl.BlockSpec(memory_space=pltpu.VMEM), pl.BlockSpec(memory_space=pltpu.SMEM)],
         out_specs=(anywhere, anywhere, anywhere),
         scratch_shapes=[
             pltpu.VMEM((slots, key_heads, 2 * tokens + DOC_ROWS, E), jnp.bfloat16),
+            pltpu.VMEM((DOC_ROWS, E), jnp.bfloat16),
             pltpu.VMEM((tokens, heads * E), jnp.bfloat16),
             pltpu.VMEM((tokens, heads * E), jnp.bfloat16),
             pltpu.VMEM((length, 2 * E), jnp.bfloat16),
@@ -288,7 +313,7 @@
             pltpu.VMEM((tokens, tokens), jnp.float32),
             pltpu.VMEM((groups_n, depth, 2, PAGE, E), jnp.bfloat16),
             pltpu.VMEM((groups_n, 8, E), jnp.float32),
-            pltpu.SemaphoreType.DMA((3 * key_heads,)),
+            pltpu.SemaphoreType.DMA((2 * key_heads + 1,)),
             pltpu.SemaphoreType.DMA,
             pltpu.SemaphoreType.DMA((key_heads,)),
             pltpu.SemaphoreType.DMA((slots, key_heads)),
@@ -303,7 +328,7 @@
         compiler_params=pltpu.CompilerParams(
             collective_id=0, has_side_effects=True, vmem_limit_bytes=56 * 1024 * 1024),
         name="attend_and_deliver",
-    )(query_rows, key_rows, value_rows, marks, owners[0, :, 0])
+    )(query_rows, key_rows, value_rows, documents, owners[0, :, 0])
     page_scales = scales[:, : 2 * depth, 0].reshape(1, groups_n * depth, 2).astype(jnp.bfloat16)
     return (attended, pool, page_scales)
 

time: 65.2 us -> 62 us (0.951)
  the two profiles are of different devices: /device:TPU:28 before, /device:TPU:26 now
where the time goes in v2:
time: 62 us; the launch traced here: 61.8 us
  Pallas kernels  55.6 us (90%)
  local copies, waits for them, and re-layouts  5.48 us (9%)
  between operations  0.64 us (1%)
    pallas_call x1, Pallas kernels, local(): pl.pallas_call(functools.partial(kernel, heads, key_heads, ctx_count, gro...  55.6 us
    unnamed x5, local copies, waits for them, and re-layouts  4.59 us

profile of v2, /device:TPU:26, one launch (start us, length us, event | category | flops | bytes accessed | tf_op | source)
XLA Modules:
  0.0 61.8 jit_solution(16048621997788978539)
XLA Ops:
  0.6 55.6 %attend_and_deliver.1 = (bf16[1,256,4096]{2,1,0:T(8,128)(2,1)}, bf16[1,8,2,128,128]{4,3,2,1,0:T(8,128)(2,1)}, f32[4,8,128]{2,1,0:T(8,128)}) custom-call(bf16[1,256,4096]{2,1,0:T(8,128)(2,1)} %query_ref.1, bf16[1,256,512]{2,1,0:T(8,128)(2,1)} %key_ref.1, bf16[1,256,512]{2,1,0:T(8,128)(2,1)} %value_ref.1, s32[1,256]{1,0:T(1,128)} %doc_ref.1, s32[8]{0:T(128)} %bitcast.1), custom_call_target="tpu_custom_call" | custom-call | tf_op jit(solution)/shard_map/attend_and_deliver/pallas_call | solution.py:295
  56.3 0.8 %fusion = bf16[4,4]{1,0:T(4,128)(2,1)S(1)} fusion(f32[4,8,128]{2,1,0:T(8,128)} %get-tuple-element.8), kind=kLoop, calls=%fused_computation.1 | loop fusion | bytes 64 | tf_op jit(solution)/shard_map/slice | solution.py:332
  57.1 0.1 convert_element_type.12
  57.2 0.6 copy.9
  57.8 0.0 copy-start
  57.8 3.2 %copy.12 = bf16[1,256,4096]{2,1,0:T(8,128)(2,1)} copy(bf16[1,256,4096]{2,1,0:T(8,128)(2,1)} %get-tuple-element.18) | data formatting | bytes 4194304
  61.0 0.0 copy-done
  61.0 0.8 %copy.13 = bf16[1,8,2,128,128]{4,3,2,1,0:T(8,128)(2,1)} copy(bf16[1,8,2,128,128]{4,3,2,1,0:T(8,128)(2,1)S(1)} %copy-done) | data formatting | bytes 1048576
Async XLA Ops:
  57.8 3.2 %copy-start = (bf16[1,8,2,128,128]{4,3,2,1,0:T(8,128)(2,1)S(1)}, bf16[1,8,2,128,128]{4,3,2,1,0:T(8,128)(2,1)}, u32[]{:S(2)}) copy-start(bf16[1,8,2,128,128]{4,3,2,1,0:T(8,128)(2,1)} %get-tuple-element.19) | copy-start | bytes 1572868
